TPU v7x, 256 devices: a whole 4x4x8 slice. The times are simulated.
256 devices in a mesh: dp: 8 (over x, z_hi), pipe: 4 (over z_lo), expert: 8 (over y, core).
Axes of the slice: x: 4, y: 4, z: 8 (z_hi: 2, z_lo: 4; z = z_hi * 4 + z_lo), core: 2. Of those that a mesh axis runs over, the one named last changes fastest.
Arguments:
- tokens: bfloat16 [8192, 2048], P(('dp', 'expert')), may hold values from -6 to 6
- cotangent: bfloat16 [8192, 2048], P(('dp', 'expert')), may hold values from -6 to 6
- owner_ids: int32 [4, 8192, 4], P('pipe', ('dp', 'expert')), may hold values from 0 to 63, all different within a row; in each aligned block of 32 rows (0 to 31, 32 to 63, ..., all dimensions but the last counted through in order) at most 3 rows name the same one
- gate_weights: bfloat16 [4, 8192, 4], P('pipe', ('dp', 'expert')), may hold values from 0.049804688 to 0.25
- norm_gain: float32 [4, 2048], P('pipe'), may hold values from 0.5 to 1.5
- w_gate: bfloat16 [4, 64, 2048, 384], P('pipe', ('dp', 'expert')), may hold values from -0.125 to 0.125
- w_up: bfloat16 [4, 64, 2048, 384], P('pipe', ('dp', 'expert')), may hold values from -0.125 to 0.125
- w_down: bfloat16 [4, 64, 384, 2048], P('pipe', ('dp', 'expert')), may hold values from -0.3125 to 0.3125
Outputs:
- segment_out: bfloat16 [4, 8192, 2048], P('pipe', ('dp', 'expert'))
- segment_grad: bfloat16 [4, 8192, 2048], P('pipe', ('dp', 'expert'))
- gain_grad: float32 [4, 2048], P('pipe')
Inputs may be any that keep to these rules, and one draw needn't show every extreme that they name: `owner_ids`: each row names 4 different owners. In each aligned block of 32 rows (layers in order, then tokens) no owner is named by more than 3 rows, and that bound is reached.
All inputs are finite; a program needn't handle non-finite values.
Results may differ from a plain program's by a relative error of at most 0.014.
Values may be sent and summed in bfloat16 or wider, within the bound.
A program may use at most 128 MiB of HBM per device.

v0:
```python
import jax
import jax.numpy as jnp
from jax import lax
from jax.sharding import PartitionSpec as P

MICRO = 4
epsilon = 1e-06


def from_behind(value, axis, steps):
    count = lax.axis_size(axis)
    leading, last = (max(0, -steps), min(count, count - steps))
    return lax.ppermute(value, axis, [(source, source + steps) for source in range(leading, last)])


def inverse_rms(values):
    return lax.rsqrt(jnp.mean(values * values, axis=-1, keepdims=True) + epsilon)


def contract_last(left, right):
    return lax.dot_general(
        left, right, (((1,), (1,)), ((), ())), preferred_element_type=jnp.float32
    )


def route_tables(ids_part, owners, capacity):
    owner_range = jnp.arange(owners, dtype=jnp.int32)
    onehot = (ids_part[:, :, None] == owner_range[None, None, :]).astype(jnp.int32)
    member = jnp.sum(onehot, axis=1)
    position = jnp.cumsum(member, axis=0) - member
    slot_range = jnp.arange(capacity, dtype=jnp.int32)
    placed = (position[:, :, None] == slot_range[None, None, :]) & (member[:, :, None] > 0)
    placing = jnp.transpose(placed, (1, 2, 0)).astype(jnp.bfloat16)
    return (onehot.astype(jnp.float32), placing)


def gate_slots(onehot, gates_part, placing, experts_here):
    gate_pairs = gates_part.astype(jnp.float32).reshape(gates_part.shape[0], -1, experts_here)
    chosen = jnp.einsum("rjo,rjc->roc", onehot, gate_pairs)
    return jnp.einsum("okr,roc->okc", placing.astype(jnp.float32), chosen).astype(jnp.bfloat16)


def send_rows(row_block, pair_block):
    got_rows, got_pairs = (
        lax.all_to_all(row_block, ("dp", "expert"), split_axis=0, concat_axis=0, tiled=True),
        lax.all_to_all(pair_block, ("dp", "expert"), split_axis=0, concat_axis=0, tiled=True),
    )
    return (got_rows, got_pairs)


def return_rows(row_block):
    return lax.all_to_all(row_block, ("dp", "expert"), split_axis=0, concat_axis=0, tiled=True)


def send_grads(row_block):
    return lax.all_to_all(row_block, ("dp", "expert"), split_axis=0, concat_axis=0, tiled=True)


def return_grads(row_block):
    return lax.all_to_all(row_block, ("dp", "expert"), split_axis=0, concat_axis=0, tiled=True)


def expert_forward(flat_rows, flat_pairs, joint_mats, down_mats):
    hidden_width = down_mats.shape[1]
    joint_pre = jnp.dot(flat_rows, joint_mats[0], preferred_element_type=jnp.float32)
    gate_pre = joint_pre[:, :hidden_width]
    up_pre = joint_pre[:, hidden_width:]
    hidden = (jax.nn.silu(gate_pre) * up_pre).astype(jnp.bfloat16)
    projected = jnp.dot(hidden, down_mats[0], preferred_element_type=jnp.float32)
    term = flat_pairs.astype(jnp.float32) * projected
    kept_both = [joint_pre]
    return (term.astype(jnp.bfloat16), jnp.stack(kept_both))


def expert_backward(grad_rows, flat_pairs, joint_keep, joint_mats, down_mats):
    hidden_width = down_mats.shape[1]
    q_vals = contract_last(grad_rows, down_mats[0])
    gate_pre = joint_keep[0][:, :hidden_width]
    up_pre = joint_keep[0][:, hidden_width:]
    sigma = jax.nn.sigmoid(gate_pre)
    weight = flat_pairs.astype(jnp.float32)
    d_gate = (q_vals * weight * up_pre * sigma * (1.0 + gate_pre * (1.0 - sigma))).astype(
        jnp.bfloat16
    )
    d_up = (q_vals * weight * gate_pre * sigma).astype(jnp.bfloat16)
    joint_grad = jnp.concatenate([d_gate, d_up], axis=1)
    term = contract_last(joint_grad, joint_mats[0])
    return term.astype(jnp.bfloat16)


def body(tokens, cotangent, owner_ids, gate_weights, norm_gain, w_gate, w_up, w_down):
    segments = lax.axis_size("pipe")
    segment_index = lax.axis_index("pipe")
    owners = lax.axis_size("dp") * lax.axis_size("expert")
    tok_rows = tokens.shape[0]
    width = tokens.shape[1]
    micro_rows = tok_rows // MICRO
    route_count = owner_ids.shape[2]
    capacity = max(2, (5 * micro_rows * route_count + 4 * owners - 1) // (4 * owners))
    slot_count = owners * capacity
    gain_row = norm_gain[0]
    joint_mats = jnp.concatenate([w_gate[0], w_up[0]], axis=2)
    down_mats = w_down[0]
    layer_ids = owner_ids[0]
    layer_gates = gate_weights[0]
    experts_here = joint_mats.shape[0]
    joint_width = joint_mats.shape[2]

    def skip_forward(operands):
        return (
            jnp.zeros((slot_count, width), jnp.bfloat16),
            jnp.zeros((experts_here, slot_count, joint_width), jnp.float32),
        )

    def run_forward(operands):
        return expert_forward(operands[0], operands[1], joint_mats, down_mats)

    def skip_backward(operands):
        return jnp.zeros((slot_count, width), jnp.bfloat16)

    def run_backward(operands):
        return expert_backward(operands[0], operands[1], operands[2], joint_mats, down_mats)

    def timing(micro):
        is_valid = (micro >= 0) & (micro < MICRO)
        slot_pick = jnp.where(is_valid, micro, MICRO)
        start_row = jnp.clip(micro, 0, MICRO - 1) * micro_rows
        return (is_valid, slot_pick, start_row)

    layer_outs = jnp.zeros((MICRO + 1, micro_rows, width), jnp.bfloat16)
    layer_ins = jnp.zeros((MICRO + 1, micro_rows, width), jnp.bfloat16)
    kept_joint = jnp.zeros((MICRO + 1, experts_here, slot_count, joint_width), jnp.float32)
    kept_pairs = jnp.zeros((MICRO + 1, slot_count, experts_here), jnp.bfloat16)
    grad_outs = jnp.zeros((MICRO + 1, micro_rows, width), jnp.bfloat16)
    gain_sum = jnp.zeros((width,), jnp.float32)
    ticks = MICRO + segments - 1
    incoming = jnp.zeros((micro_rows, width), jnp.bfloat16)
    for tick_num in range(ticks):
        forward_is_valid, forward_slot_pick, forward_start_row = timing(tick_num - segment_index)
        forward_own_part = lax.dynamic_slice_in_dim(tokens, forward_start_row, micro_rows, 0)
        forward_layer_in = jnp.where(segment_index == 0, forward_own_part, incoming)
        forward_ids_part = lax.dynamic_slice_in_dim(layer_ids, forward_start_row, micro_rows, 0)
        gates_part = lax.dynamic_slice_in_dim(layer_gates, forward_start_row, micro_rows, 0)
        forward_x_float = forward_layer_in.astype(jnp.float32)
        forward_scale = inverse_rms(forward_x_float)
        normed = (forward_x_float * forward_scale * gain_row).astype(jnp.bfloat16)
        forward_onehot, forward_placing = route_tables(forward_ids_part, owners, capacity)
        row_block = jnp.einsum(
            "okr,rd->okd", forward_placing, normed, preferred_element_type=jnp.float32
        ).astype(jnp.bfloat16)
        pair_block = gate_slots(forward_onehot, gates_part, forward_placing, experts_here)
        f_valid, f_pick, layer_in, x_float, f_placing, row_block, pair_block = (
            forward_is_valid,
            forward_slot_pick,
            forward_layer_in,
            forward_x_float,
            forward_placing,
            row_block,
            pair_block,
        )
        got_rows, got_pairs = send_rows(row_block, pair_block)
        flat_rows = got_rows.reshape(slot_count, width)
        flat_pairs = got_pairs.reshape(slot_count, experts_here)
        result, joint_pre = lax.cond(f_valid, run_forward, skip_forward, (flat_rows, flat_pairs))
        returned = return_rows(result.reshape(owners, capacity, width))
        branch = jnp.einsum("okr,okd->rd", f_placing, returned, preferred_element_type=jnp.float32)
        layer_out = (x_float + branch).astype(jnp.bfloat16)
        layer_outs = lax.dynamic_update_index_in_dim(layer_outs, layer_out, f_pick, 0)
        layer_ins = lax.dynamic_update_index_in_dim(layer_ins, layer_in, f_pick, 0)
        kept_joint = lax.dynamic_update_index_in_dim(kept_joint, joint_pre, f_pick, 0)
        kept_pairs = lax.dynamic_update_index_in_dim(kept_pairs, flat_pairs, f_pick, 0)
        if tick_num + 1 < ticks:
            incoming = from_behind(layer_out, "pipe", 1)
    incoming = jnp.zeros((micro_rows, width), jnp.bfloat16)
    for tick_num in range(ticks):
        backward_is_valid, backward_slot_pick, backward_start_row = timing(
            tick_num - (segments - 1 - segment_index)
        )
        own_part = lax.dynamic_slice_in_dim(cotangent, backward_start_row, micro_rows, 0)
        backward_grad_in = jnp.where(segment_index == segments - 1, own_part, incoming)
        ids_part = lax.dynamic_slice_in_dim(layer_ids, backward_start_row, micro_rows, 0)
        backward_layer_in = lax.dynamic_index_in_dim(
            layer_ins, backward_slot_pick, 0, keepdims=False
        )
        backward_x_float = backward_layer_in.astype(jnp.float32)
        backward_scale = inverse_rms(backward_x_float)
        onehot, backward_placing = route_tables(ids_part, owners, capacity)
        grad_block = jnp.einsum(
            "okr,rd->okd", backward_placing, backward_grad_in, preferred_element_type=jnp.float32
        ).astype(jnp.bfloat16)
        b_valid, b_pick, grad_in, bx_float, b_scale, b_placing, grad_block = (
            backward_is_valid,
            backward_slot_pick,
            backward_grad_in,
            backward_x_float,
            backward_scale,
            backward_placing,
            grad_block,
        )
        got_grads = send_grads(grad_block).reshape(slot_count, width)
        joint_keep = lax.dynamic_index_in_dim(kept_joint, b_pick, 0, keepdims=False)
        pair_keep = lax.dynamic_index_in_dim(kept_pairs, b_pick, 0, keepdims=False)
        owner_grad = lax.cond(
            b_valid, run_backward, skip_backward, (got_grads, pair_keep, joint_keep)
        )
        returned = return_grads(owner_grad.reshape(owners, capacity, width))
        normed_grad = jnp.einsum(
            "okr,okd->rd", b_placing, returned, preferred_element_type=jnp.float32
        )
        weighted = gain_row * normed_grad
        grad_x = (
            grad_in.astype(jnp.float32)
            + b_scale * weighted
            - bx_float
            * b_scale
            * b_scale
            * b_scale
            * jnp.mean(weighted * bx_float, axis=-1, keepdims=True)
        )
        gain_term = jnp.where(b_valid, jnp.sum(normed_grad * bx_float * b_scale, axis=0), 0.0)
        grad_bf, gain_term = (grad_x.astype(jnp.bfloat16), gain_term)
        grad_outs = lax.dynamic_update_index_in_dim(grad_outs, grad_bf, b_pick, 0)
        gain_sum = gain_sum + gain_term
        if tick_num + 1 < ticks:
            incoming = from_behind(grad_bf, "pipe", -1)
    gain_grad = lax.psum(gain_sum, ("dp", "expert"))
    segment_out = layer_outs[:MICRO].reshape(1, tok_rows, width)
    segment_grad = grad_outs[:MICRO].reshape(1, tok_rows, width)
    return (segment_out, segment_grad, gain_grad.reshape(1, width))


def solution(mesh):
    in_specs = (
        P(("dp", "expert"), None),
        P(("dp", "expert"), None),
        P("pipe", ("dp", "expert"), None),
        P("pipe", ("dp", "expert"), None),
        P("pipe", None),
        P("pipe", ("dp", "expert"), None, None),
        P("pipe", ("dp", "expert"), None, None),
        P("pipe", ("dp", "expert"), None, None),
    )
    out_specs = (
        P("pipe", ("dp", "expert"), None),
        P("pipe", ("dp", "expert"), None),
        P("pipe", None),
    )
    return jax.shard_map(body, mesh=mesh, in_specs=in_specs, out_specs=out_specs, check_vma=False)
```

profile of v0, /device:TPU:1, one launch (start us, length us, event | category | flops | bytes accessed | tf_op | source)
XLA Modules:
  0.0 1507.8 jit_solution(17595029229092546663)
XLA Ops:
  40.4 25.5 %all-to-all-done.1 = bf16[64,3,2048]{2,1,0:T(4,128)(2,1)} async-done(((bf16[64,3,2048]{2,1,0:T(4,128)(2,1)}), bf16[64,3,2048]{2,1,0:T(4,128)(2,1)}, u32[]{:S(2)}, u32[]{:S(2)}) %all-to-all-start.1) | async-done | bytes 786464 | tf_op jit(solution)/shard_map/all_to_all | solution.py:45
  136.9 28.5 %all-to-all-done.4 = bf16[64,3,2048]{2,1,0:T(4,128)(2,1)} async-done(((bf16[64,3,2048]{2,1,0:T(4,128)(2,1)}), bf16[64,3,2048]{2,1,0:T(4,128)(2,1)}, u32[]{:S(2)}, u32[]{:S(2)}) %all-to-all-start.4) | async-done | bytes 786464 | tf_op jit(solution)/shard_map/all_to_all | solution.py:45
  246.7 28.6 %all-to-all-done.7 = bf16[64,3,2048]{2,1,0:T(4,128)(2,1)} async-done(((bf16[64,3,2048]{2,1,0:T(4,128)(2,1)}), bf16[64,3,2048]{2,1,0:T(4,128)(2,1)}, u32[]{:S(2)}, u32[]{:S(2)}) %all-to-all-start.7) | async-done | bytes 786464 | tf_op jit(solution)/shard_map/all_to_all | solution.py:45
  298.6 20.2 %all-to-all-done.8 = bf16[64,3,2048]{2,1,0:T(4,128)(2,1)} async-done(((bf16[64,3,2048]{2,1,0:T(4,128)(2,1)}), bf16[64,3,2048]{2,1,0:T(4,128)(2,1)}, u32[]{:S(2)}, u32[]{:S(2)}) %all-to-all-start.8) | async-done | bytes 786464 | tf_op jit(solution)/shard_map/all_to_all | solution.py:52
  350.9 26.9 %all-to-all-done.10 = bf16[64,3,2048]{2,1,0:T(4,128)(2,1)} async-done(((bf16[64,3,2048]{2,1,0:T(4,128)(2,1)}), bf16[64,3,2048]{2,1,0:T(4,128)(2,1)}, u32[]{:S(2)}, u32[]{:S(2)}) %all-to-all-start.10) | async-done | bytes 786464 | tf_op jit(solution)/shard_map/all_to_all | solution.py:45
  399.7 21.5 %all-to-all-done.11 = bf16[64,3,2048]{2,1,0:T(4,128)(2,1)} async-done(((bf16[64,3,2048]{2,1,0:T(4,128)(2,1)}), bf16[64,3,2048]{2,1,0:T(4,128)(2,1)}, u32[]{:S(2)}, u32[]{:S(2)}) %all-to-all-start.11) | async-done | bytes 786464 | tf_op jit(solution)/shard_map/all_to_all | solution.py:52
  452.8 21.8 %all-to-all-done.13 = bf16[64,3,2048]{2,1,0:T(4,128)(2,1)} async-done(((bf16[64,3,2048]{2,1,0:T(4,128)(2,1)}), bf16[64,3,2048]{2,1,0:T(4,128)(2,1)}, u32[]{:S(2)}, u32[]{:S(2)}) %all-to-all-start.13) | async-done | bytes 786464 | tf_op jit(solution)/shard_map/all_to_all | solution.py:45
  486.5 24.1 %all-to-all-done.14 = bf16[64,3,2048]{2,1,0:T(4,128)(2,1)} async-done(((bf16[64,3,2048]{2,1,0:T(4,128)(2,1)}), bf16[64,3,2048]{2,1,0:T(4,128)(2,1)}, u32[]{:S(2)}, u32[]{:S(2)}) %all-to-all-start.14) | async-done | bytes 786464 | tf_op jit(solution)/shard_map/all_to_all | solution.py:52
  542.1 22.4 %all-to-all-done.16 = bf16[64,3,2048]{2,1,0:T(4,128)(2,1)} async-done(((bf16[64,3,2048]{2,1,0:T(4,128)(2,1)}), bf16[64,3,2048]{2,1,0:T(4,128)(2,1)}, u32[]{:S(2)}, u32[]{:S(2)}) %all-to-all-start.16) | async-done | bytes 786464 | tf_op jit(solution)/shard_map/all_to_all | solution.py:45
  580.6 26.7 %all-to-all-done.17 = bf16[64,3,2048]{2,1,0:T(4,128)(2,1)} async-done(((bf16[64,3,2048]{2,1,0:T(4,128)(2,1)}), bf16[64,3,2048]{2,1,0:T(4,128)(2,1)}, u32[]{:S(2)}, u32[]{:S(2)}) %all-to-all-start.17) | async-done | bytes 786464 | tf_op jit(solution)/shard_map/all_to_all | solution.py:52
  642.5 23.4 %all-to-all-done.19 = bf16[64,3,2048]{2,1,0:T(4,128)(2,1)} async-done(((bf16[64,3,2048]{2,1,0:T(4,128)(2,1)}), bf16[64,3,2048]{2,1,0:T(4,128)(2,1)}, u32[]{:S(2)}, u32[]{:S(2)}) %all-to-all-start.19) | async-done | bytes 786464 | tf_op jit(solution)/shard_map/all_to_all | solution.py:45
  701.7 20.6 %all-to-all-done.22 = bf16[64,3,2048]{2,1,0:T(4,128)(2,1)} async-done(((bf16[64,3,2048]{2,1,0:T(4,128)(2,1)}), bf16[64,3,2048]{2,1,0:T(4,128)(2,1)}, u32[]{:S(2)}, u32[]{:S(2)}) %all-to-all-start.22) | async-done | bytes 786464 | tf_op jit(solution)/shard_map/all_to_all | solution.py:60
  750.4 28.5 %all-to-all-done.23 = bf16[64,3,2048]{2,1,0:T(4,128)(2,1)} async-done(((bf16[64,3,2048]{2,1,0:T(4,128)(2,1)}), bf16[64,3,2048]{2,1,0:T(4,128)(2,1)}, u32[]{:S(2)}, u32[]{:S(2)}) %all-to-all-start.23) | async-done | bytes 786464 | tf_op jit(solution)/shard_map/all_to_all | solution.py:56
  788.4 19.0 %all-to-all-done.24 = bf16[64,3,2048]{2,1,0:T(4,128)(2,1)} async-done(((bf16[64,3,2048]{2,1,0:T(4,128)(2,1)}), bf16[64,3,2048]{2,1,0:T(4,128)(2,1)}, u32[]{:S(2)}, u32[]{:S(2)}) %all-to-all-start.24) | async-done | bytes 786464 | tf_op jit(solution)/shard_map/all_to_all | solution.py:60
  839.6 28.5 %all-to-all-done.25 = bf16[64,3,2048]{2,1,0:T(4,128)(2,1)} async-done(((bf16[64,3,2048]{2,1,0:T(4,128)(2,1)}), bf16[64,3,2048]{2,1,0:T(4,128)(2,1)}, u32[]{:S(2)}, u32[]{:S(2)}) %all-to-all-start.25) | async-done | bytes 786464 | tf_op jit(solution)/shard_map/all_to_all | solution.py:56
  877.8 19.0 %all-to-all-done.26 = bf16[64,3,2048]{2,1,0:T(4,128)(2,1)} async-done(((bf16[64,3,2048]{2,1,0:T(4,128)(2,1)}), bf16[64,3,2048]{2,1,0:T(4,128)(2,1)}, u32[]{:S(2)}, u32[]{:S(2)}) %all-to-all-start.26) | async-done | bytes 786464 | tf_op jit(solution)/shard_map/all_to_all | solution.py:60
  930.2 28.5 %all-to-all-done.27 = bf16[64,3,2048]{2,1,0:T(4,128)(2,1)} async-done(((bf16[64,3,2048]{2,1,0:T(4,128)(2,1)}), bf16[64,3,2048]{2,1,0:T(4,128)(2,1)}, u32[]{:S(2)}, u32[]{:S(2)}) %all-to-all-start.27) | async-done | bytes 786464 | tf_op jit(solution)/shard_map/all_to_all | solution.py:56
  976.9 19.1 %all-to-all-done.28 = bf16[64,3,2048]{2,1,0:T(4,128)(2,1)} async-done(((bf16[64,3,2048]{2,1,0:T(4,128)(2,1)}), bf16[64,3,2048]{2,1,0:T(4,128)(2,1)}, u32[]{:S(2)}, u32[]{:S(2)}) %all-to-all-start.28) | async-done | bytes 786464 | tf_op jit(solution)/shard_map/all_to_all | solution.py:60
  1020.2 28.5 %all-to-all-done.29 = bf16[64,3,2048]{2,1,0:T(4,128)(2,1)} async-done(((bf16[64,3,2048]{2,1,0:T(4,128)(2,1)}), bf16[64,3,2048]{2,1,0:T(4,128)(2,1)}, u32[]{:S(2)}, u32[]{:S(2)}) %all-to-all-start.29) | async-done | bytes 786464 | tf_op jit(solution)/shard_map/all_to_all | solution.py:56
  1066.9 19.1 %all-to-all-done.30 = bf16[64,3,2048]{2,1,0:T(4,128)(2,1)} async-done(((bf16[64,3,2048]{2,1,0:T(4,128)(2,1)}), bf16[64,3,2048]{2,1,0:T(4,128)(2,1)}, u32[]{:S(2)}, u32[]{:S(2)}) %all-to-all-start.30) | async-done | bytes 786464 | tf_op jit(solution)/shard_map/all_to_all | solution.py:60
  1091.4 23.4 %collective-permute-done.10 = bf16[32,2048]{1,0:T(8,128)(2,1)S(1)} collective-permute-done((bf16[32,2048]{1,0:T(8,128)(2,1)S(1)}, bf16[32,2048]{1,0:T(8,128)(2,1)S(1)}, u32[]{:S(2)}, u32[]{:S(2)}) %collective-permute-start.10) | collective-permute-done | bytes 131104 | tf_op jit(solution)/shard_map/ppermute | solution.py:13
  1123.6 28.0 %all-to-all-done.31 = bf16[64,3,2048]{2,1,0:T(4,128)(2,1)} async-done(((bf16[64,3,2048]{2,1,0:T(4,128)(2,1)}), bf16[64,3,2048]{2,1,0:T(4,128)(2,1)}, u32[]{:S(2)}, u32[]{:S(2)}) %all-to-all-start.31) | async-done | bytes 786464 | tf_op jit(solution)/shard_map/all_to_all | solution.py:56
  1170.2 27.8 %all-to-all-done.32 = bf16[64,3,2048]{2,1,0:T(4,128)(2,1)} async-done(((bf16[64,3,2048]{2,1,0:T(4,128)(2,1)}), bf16[64,3,2048]{2,1,0:T(4,128)(2,1)}, u32[]{:S(2)}, u32[]{:S(2)}) %all-to-all-start.32) | async-done | bytes 786464 | tf_op jit(solution)/shard_map/all_to_all | solution.py:60
  1302.3 203.1 %psum.7 = f32[1,2048]{1,0:T(1,128)} all-reduce(f32[1,2048]{1,0:T(1,128)S(1)} %bitcast.633), channel_id=1, replica_groups=mesh['dp'=8,'pipe'=4,'expert'=8] {'dp','expert'}, use_global_device_ids=true, to_apply=%region_84.85 | all-reduce | flops 2048 | bytes 16384 | tf_op jit(solution)/shard_map/psum | solution.py:226
  (416 shorter events, 826.0 us)
Async XLA Ops:
  5.5 27.2 %all-to-all-start = ((bf16[64,3,1]{1,2,0:T(2,128)(2,1)}), bf16[64,3,1]{1,2,0:T(2,128)(2,1)S(1)}, u32[]{:S(2)}, u32[]{:S(2)}) async-start(bf16[64,3,1]{1,2,0:T(2,128)(2,1)} %copy.214), calls=%async_computation | async-start | bytes 65536 | tf_op jit(solution)/shard_map/all_to_all | solution.py:46
  32.7 33.2 %all-to-all-start.1 = ((bf16[64,3,2048]{2,1,0:T(4,128)(2,1)}), bf16[64,3,2048]{2,1,0:T(4,128)(2,1)}, u32[]{:S(2)}, u32[]{:S(2)}) async-start(bf16[64,3,2048]{2,1,0:T(4,128)(2,1)} %copy.215), calls=%async_computation.1 | async-start | bytes 2097152 | tf_op jit(solution)/shard_map/all_to_all | solution.py:45
  78.3 24.5 %all-to-all-start.2 = ((bf16[64,3,2048]{2,1,0:T(4,128)(2,1)}), bf16[64,3,2048]{2,1,0:T(4,128)(2,1)}, u32[]{:S(2)}, u32[]{:S(2)}) async-start(bf16[64,3,2048]{2,1,0:T(4,128)(2,1)} %reshape.639), calls=%async_computation.2 | async-start | bytes 2097152 | tf_op jit(solution)/shard_map/all_to_all | solution.py:52
  122.4 43.0 %all-to-all-start.4 = ((bf16[64,3,2048]{2,1,0:T(4,128)(2,1)}), bf16[64,3,2048]{2,1,0:T(4,128)(2,1)}, u32[]{:S(2)}, u32[]{:S(2)}) async-start(bf16[64,3,2048]{2,1,0:T(4,128)(2,1)} %copy.219), calls=%async_computation.4 | async-start | bytes 2097152 | tf_op jit(solution)/shard_map/all_to_all | solution.py:45
  240.8 34.5 %all-to-all-start.7 = ((bf16[64,3,2048]{2,1,0:T(4,128)(2,1)}), bf16[64,3,2048]{2,1,0:T(4,128)(2,1)}, u32[]{:S(2)}, u32[]{:S(2)}) async-start(bf16[64,3,2048]{2,1,0:T(4,128)(2,1)} %copy.223), calls=%async_computation.7 | async-start | bytes 2097152 | tf_op jit(solution)/shard_map/all_to_all | solution.py:45
  287.7 31.1 %all-to-all-start.8 = ((bf16[64,3,2048]{2,1,0:T(4,128)(2,1)}), bf16[64,3,2048]{2,1,0:T(4,128)(2,1)}, u32[]{:S(2)}, u32[]{:S(2)}) async-start(bf16[64,3,2048]{2,1,0:T(4,128)(2,1)} %reshape.643), calls=%async_computation.8 | async-start | bytes 2097152 | tf_op jit(solution)/shard_map/all_to_all | solution.py:52
  345.1 32.7 %all-to-all-start.10 = ((bf16[64,3,2048]{2,1,0:T(4,128)(2,1)}), bf16[64,3,2048]{2,1,0:T(4,128)(2,1)}, u32[]{:S(2)}, u32[]{:S(2)}) async-start(bf16[64,3,2048]{2,1,0:T(4,128)(2,1)} %copy.227), calls=%async_computation.10 | async-start | bytes 2097152 | tf_op jit(solution)/shard_map/all_to_all | solution.py:45
  390.2 31.1 %all-to-all-start.11 = ((bf16[64,3,2048]{2,1,0:T(4,128)(2,1)}), bf16[64,3,2048]{2,1,0:T(4,128)(2,1)}, u32[]{:S(2)}, u32[]{:S(2)}) async-start(bf16[64,3,2048]{2,1,0:T(4,128)(2,1)} %reshape.645), calls=%async_computation.11 | async-start | bytes 2097152 | tf_op jit(solution)/shard_map/all_to_all | solution.py:52
  447.0 27.6 %all-to-all-start.13 = ((bf16[64,3,2048]{2,1,0:T(4,128)(2,1)}), bf16[64,3,2048]{2,1,0:T(4,128)(2,1)}, u32[]{:S(2)}, u32[]{:S(2)}) async-start(bf16[64,3,2048]{2,1,0:T(4,128)(2,1)} %copy.231), calls=%async_computation.13 | async-start | bytes 2097152 | tf_op jit(solution)/shard_map/all_to_all | solution.py:45
  479.9 30.7 %all-to-all-start.14 = ((bf16[64,3,2048]{2,1,0:T(4,128)(2,1)}), bf16[64,3,2048]{2,1,0:T(4,128)(2,1)}, u32[]{:S(2)}, u32[]{:S(2)}) async-start(bf16[64,3,2048]{2,1,0:T(4,128)(2,1)} %reshape.647), calls=%async_computation.14 | async-start | bytes 2097152 | tf_op jit(solution)/shard_map/all_to_all | solution.py:52
  536.3 28.2 %all-to-all-start.16 = ((bf16[64,3,2048]{2,1,0:T(4,128)(2,1)}), bf16[64,3,2048]{2,1,0:T(4,128)(2,1)}, u32[]{:S(2)}, u32[]{:S(2)}) async-start(bf16[64,3,2048]{2,1,0:T(4,128)(2,1)} %copy.235), calls=%async_computation.16 | async-start | bytes 2097152 | tf_op jit(solution)/shard_map/all_to_all | solution.py:45
  569.6 37.7 %all-to-all-start.17 = ((bf16[64,3,2048]{2,1,0:T(4,128)(2,1)}), bf16[64,3,2048]{2,1,0:T(4,128)(2,1)}, u32[]{:S(2)}, u32[]{:S(2)}) async-start(bf16[64,3,2048]{2,1,0:T(4,128)(2,1)} %reshape.649), calls=%async_computation.17 | async-start | bytes 2097152 | tf_op jit(solution)/shard_map/all_to_all | solution.py:52
  631.6 34.4 %all-to-all-start.19 = ((bf16[64,3,2048]{2,1,0:T(4,128)(2,1)}), bf16[64,3,2048]{2,1,0:T(4,128)(2,1)}, u32[]{:S(2)}, u32[]{:S(2)}) async-start(bf16[64,3,2048]{2,1,0:T(4,128)(2,1)} %copy.239), calls=%async_computation.19 | async-start | bytes 2097152 | tf_op jit(solution)/shard_map/all_to_all | solution.py:45
  694.6 27.6 %all-to-all-start.22 = ((bf16[64,3,2048]{2,1,0:T(4,128)(2,1)}), bf16[64,3,2048]{2,1,0:T(4,128)(2,1)}, u32[]{:S(2)}, u32[]{:S(2)}) async-start(bf16[64,3,2048]{2,1,0:T(4,128)(2,1)} %reshape.654), calls=%async_computation.22 | async-start | bytes 2097152 | tf_op jit(solution)/shard_map/all_to_all | solution.py:60
  744.6 34.2 %all-to-all-start.23 = ((bf16[64,3,2048]{2,1,0:T(4,128)(2,1)}), bf16[64,3,2048]{2,1,0:T(4,128)(2,1)}, u32[]{:S(2)}, u32[]{:S(2)}) async-start(bf16[64,3,2048]{2,1,0:T(4,128)(2,1)} %copy.251), calls=%async_computation.23 | async-start | bytes 2097152 | tf_op jit(solution)/shard_map/all_to_all | solution.py:56
  827.4 40.7 %all-to-all-start.25 = ((bf16[64,3,2048]{2,1,0:T(4,128)(2,1)}), bf16[64,3,2048]{2,1,0:T(4,128)(2,1)}, u32[]{:S(2)}, u32[]{:S(2)}) async-start(bf16[64,3,2048]{2,1,0:T(4,128)(2,1)} %copy.253), calls=%async_computation.25 | async-start | bytes 2097152 | tf_op jit(solution)/shard_map/all_to_all | solution.py:56
  922.4 36.3 %all-to-all-start.27 = ((bf16[64,3,2048]{2,1,0:T(4,128)(2,1)}), bf16[64,3,2048]{2,1,0:T(4,128)(2,1)}, u32[]{:S(2)}, u32[]{:S(2)}) async-start(bf16[64,3,2048]{2,1,0:T(4,128)(2,1)} %copy.255), calls=%async_computation.27 | async-start | bytes 2097152 | tf_op jit(solution)/shard_map/all_to_all | solution.py:56
  1012.4 36.3 %all-to-all-start.29 = ((bf16[64,3,2048]{2,1,0:T(4,128)(2,1)}), bf16[64,3,2048]{2,1,0:T(4,128)(2,1)}, u32[]{:S(2)}, u32[]{:S(2)}) async-start(bf16[64,3,2048]{2,1,0:T(4,128)(2,1)} %copy.257), calls=%async_computation.29 | async-start | bytes 2097152 | tf_op jit(solution)/shard_map/all_to_all | solution.py:56
  1090.1 24.7 %collective-permute-start.10 = (bf16[32,2048]{1,0:T(8,128)(2,1)S(1)}, bf16[32,2048]{1,0:T(8,128)(2,1)S(1)}, u32[]{:S(2)}, u32[]{:S(2)}) collective-permute-start(bf16[32,2048]{1,0:T(8,128)(2,1)S(1)} %get-tuple-element.782), channel_id=1, source_target_pairs={{8,0},{16,8},{24,16},{9,1},{17,9},{25,17},{10,2},{18,10},{26,18},{... | collective-permute-start | bytes 393224 | tf_op jit(solution)/shard_map/ppermute | solution.py:13
  1117.9 33.7 %all-to-all-start.31 = ((bf16[64,3,2048]{2,1,0:T(4,128)(2,1)}), bf16[64,3,2048]{2,1,0:T(4,128)(2,1)}, u32[]{:S(2)}, u32[]{:S(2)}) async-start(bf16[64,3,2048]{2,1,0:T(4,128)(2,1)} %copy.259), calls=%async_computation.31 | async-start | bytes 2097152 | tf_op jit(solution)/shard_map/all_to_all | solution.py:56
  1164.6 33.5 %all-to-all-start.32 = ((bf16[64,3,2048]{2,1,0:T(4,128)(2,1)}), bf16[64,3,2048]{2,1,0:T(4,128)(2,1)}, u32[]{:S(2)}, u32[]{:S(2)}) async-start(bf16[64,3,2048]{2,1,0:T(4,128)(2,1)} %reshape.664), calls=%async_computation.32 | async-start | bytes 2097152 | tf_op jit(solution)/shard_map/all_to_all | solution.py:60
  1211.5 31.9 %all-to-all-start.33 = ((bf16[64,3,2048]{2,1,0:T(4,128)(2,1)}), bf16[64,3,2048]{2,1,0:T(4,128)(2,1)}, u32[]{:S(2)}, u32[]{:S(2)}) async-start(bf16[64,3,2048]{2,1,0:T(4,128)(2,1)} %copy.261), calls=%async_computation.33 | async-start | bytes 2097152 | tf_op jit(solution)/shard_map/all_to_all | solution.py:56
  1243.3 29.7 %all-to-all-start.20 = ((bf16[64,3,2048]{2,1,0:T(4,128)(2,1)}), bf16[64,3,2048]{2,1,0:T(4,128)(2,1)}, u32[]{:S(2)}, u32[]{:S(2)}) async-start(bf16[64,3,2048]{2,1,0:T(4,128)(2,1)} %reshape.651), calls=%async_computation.20 | async-start | bytes 2097152 | tf_op jit(solution)/shard_map/all_to_all | solution.py:52
  1273.1 27.2 %all-to-all-start.34 = ((bf16[64,3,2048]{2,1,0:T(4,128)(2,1)}), bf16[64,3,2048]{2,1,0:T(4,128)(2,1)S(1)}, u32[]{:S(2)}, u32[]{:S(2)}) async-start(bf16[64,3,2048]{2,1,0:T(4,128)(2,1)} %reshape.666), calls=%async_computation.34 | async-start | bytes 2097152 | tf_op jit(solution)/shard_map/all_to_all | solution.py:60
  (51 other events, 836.2 us)
where the time goes:
time: 1520 us; the launch traced here: 1510 us
  waiting for transfers between devices  747 us (49%)
  starting transfers between devices  290 us (19%)
  blocking collectives  203 us (13%)
  local copies, waits for them, and re-layouts  141 us (9%)
  matrix products  92.5 us (6%)
  other arithmetic  31.6 us (2%)
    psum x1, blocking collectives, body(): gain_grad = lax.psum(gain_sum, ('dp', 'expert'))  203 us
    all_to_all x7, waiting for transfers between devices, send_rows(): lax.all_to_all(row_block, ('dp', 'expert'), split_axis=0, concat_axis=0,...  177 us
    all_to_all x7, waiting for transfers between devices, send_grads(): lax.all_to_all(row_block, ('dp', 'expert'), split_axis=0, concat_axis=0,...  165 us
    all_to_all x7, waiting for transfers between devices, return_grads(): lax.all_to_all(row_block, ('dp', 'expert'), split_axis=0, concat_axis=0,...  144 us
    all_to_all x7, waiting for transfers between devices, return_rows(): lax.all_to_all(row_block, ('dp', 'expert'), split_axis=0, concat_axis=0,...  138 us
    ppermute x12, waiting for transfers between devices, from_behind(): lax.ppermute(value, axis, [(source, source + steps) for source in range(l...  79.9 us
    all_to_all x7, starting transfers between devices, send_rows(): lax.all_to_all(pair_block, ('dp', 'expert'), split_axis=0, concat_axis=0,...  58 us
    all_to_all x7, starting transfers between devices, send_grads(): lax.all_to_all(row_block, ('dp', 'expert'), split_axis=0, concat_axis=0,...  54.3 us
  transfers between devices with their start and end apart: 47, of which 41 were waited for; matrix products, arithmetic and copies ran while one was open for 5% of the time, Pallas kernels for 0%

commit v1 on v0

--- a/solution.py
+++ b/solution.py
@@ -223,7 +223,7 @@
         gain_sum = gain_sum + gain_term
         if tick_num + 1 < ticks:
             incoming = from_behind(grad_bf, "pipe", -1)
-    gain_grad = lax.psum(gain_sum, ("dp", "expert"))
+    gain_grad = jnp.sum(lax.all_gather(gain_sum, ("dp", "expert")), axis=0)
     segment_out = layer_outs[:MICRO].reshape(1, tok_rows, width)
     segment_grad = grad_outs[:MICRO].reshape(1, tok_rows, width)
     return (segment_out, segment_grad, gain_grad.reshape(1, width))

time: 1520 us -> 1430 us (0.941)
  blocking collectives: 203 us -> 111 us
    psum x1 -> x0, blocking collectives: 203 us -> none  [body(): gain_grad = lax.psum(gain_sum, ('dp', 'expert'))]
    all_gather x0 -> x1, blocking collectives: none -> 111 us  [body(): gain_grad = jnp.sum(lax.all_gather(gain_sum, ('dp', 'expert')), axis=0)]
  transfers between devices with their start and end apart: 47 -> 47, of which waited for: 41 -> 41; matrix products, arithmetic and copies ran while one was open for 5% -> 6% of each run, Pallas kernels for 0% -> 0%
where the time goes in v1:
time: 1430 us; the launch traced here: 1420 us
  waiting for transfers between devices  747 us (52%)
  starting transfers between devices  290 us (20%)
  local copies, waits for them, and re-layouts  141 us (10%)
  blocking collectives  111 us (8%)
  matrix products  92.5 us (6%)
  other arithmetic  32.3 us (2%)
    all_to_all x7, waiting for transfers between devices, send_rows(): lax.all_to_all(row_block, ('dp', 'expert'), split_axis=0, concat_axis=0,...  177 us
    all_to_all x7, waiting for transfers between devices, send_grads(): lax.all_to_all(row_block, ('dp', 'expert'), split_axis=0, concat_axis=0,...  165 us
    all_to_all x7, waiting for transfers between devices, return_grads(): lax.all_to_all(row_block, ('dp', 'expert'), split_axis=0, concat_axis=0,...  144 us
    all_to_all x7, waiting for transfers between devices, return_rows(): lax.all_to_all(row_block, ('dp', 'expert'), split_axis=0, concat_axis=0,...  138 us
    all_gather x1, blocking collectives, body(): gain_grad = jnp.sum(lax.all_gather(gain_sum, ('dp', 'expert')), axis=0)  111 us
    ppermute x12, waiting for transfers between devices, from_behind(): lax.ppermute(value, axis, [(source, source + steps) for source in range(l...  79.9 us
    all_to_all x7, starting transfers between devices, send_rows(): lax.all_to_all(pair_block, ('dp', 'expert'), split_axis=0, concat_axis=0,...  58 us
    all_to_all x7, starting transfers between devices, send_grads(): lax.all_to_all(row_block, ('dp', 'expert'), split_axis=0, concat_axis=0,...  54.3 us
  transfers between devices with their start and end apart: 47, of which 41 were waited for; matrix products, arithmetic and copies ran while one was open for 6% of the time, Pallas kernels for 0%

profile of v1, /device:TPU:1, one launch (start us, length us, event | category | flops | bytes accessed | tf_op | source)
XLA Modules:
  0.0 1416.8 jit_solution(5256557095046495706)
XLA Ops:
  40.4 25.5 %all-to-all-done.1 = bf16[64,3,2048]{2,1,0:T(4,128)(2,1)} async-done(((bf16[64,3,2048]{2,1,0:T(4,128)(2,1)}), bf16[64,3,2048]{2,1,0:T(4,128)(2,1)}, u32[]{:S(2)}, u32[]{:S(2)}) %all-to-all-start.1) | async-done | bytes 786464 | tf_op jit(solution)/shard_map/all_to_all | solution.py:45
  136.9 28.5 %all-to-all-done.4 = bf16[64,3,2048]{2,1,0:T(4,128)(2,1)} async-done(((bf16[64,3,2048]{2,1,0:T(4,128)(2,1)}), bf16[64,3,2048]{2,1,0:T(4,128)(2,1)}, u32[]{:S(2)}, u32[]{:S(2)}) %all-to-all-start.4) | async-done | bytes 786464 | tf_op jit(solution)/shard_map/all_to_all | solution.py:45
  246.7 28.6 %all-to-all-done.7 = bf16[64,3,2048]{2,1,0:T(4,128)(2,1)} async-done(((bf16[64,3,2048]{2,1,0:T(4,128)(2,1)}), bf16[64,3,2048]{2,1,0:T(4,128)(2,1)}, u32[]{:S(2)}, u32[]{:S(2)}) %all-to-all-start.7) | async-done | bytes 786464 | tf_op jit(solution)/shard_map/all_to_all | solution.py:45
  298.6 20.2 %all-to-all-done.8 = bf16[64,3,2048]{2,1,0:T(4,128)(2,1)} async-done(((bf16[64,3,2048]{2,1,0:T(4,128)(2,1)}), bf16[64,3,2048]{2,1,0:T(4,128)(2,1)}, u32[]{:S(2)}, u32[]{:S(2)}) %all-to-all-start.8) | async-done | bytes 786464 | tf_op jit(solution)/shard_map/all_to_all | solution.py:52
  350.9 26.9 %all-to-all-done.10 = bf16[64,3,2048]{2,1,0:T(4,128)(2,1)} async-done(((bf16[64,3,2048]{2,1,0:T(4,128)(2,1)}), bf16[64,3,2048]{2,1,0:T(4,128)(2,1)}, u32[]{:S(2)}, u32[]{:S(2)}) %all-to-all-start.10) | async-done | bytes 786464 | tf_op jit(solution)/shard_map/all_to_all | solution.py:45
  399.7 21.5 %all-to-all-done.11 = bf16[64,3,2048]{2,1,0:T(4,128)(2,1)} async-done(((bf16[64,3,2048]{2,1,0:T(4,128)(2,1)}), bf16[64,3,2048]{2,1,0:T(4,128)(2,1)}, u32[]{:S(2)}, u32[]{:S(2)}) %all-to-all-start.11) | async-done | bytes 786464 | tf_op jit(solution)/shard_map/all_to_all | solution.py:52
  452.8 21.8 %all-to-all-done.13 = bf16[64,3,2048]{2,1,0:T(4,128)(2,1)} async-done(((bf16[64,3,2048]{2,1,0:T(4,128)(2,1)}), bf16[64,3,2048]{2,1,0:T(4,128)(2,1)}, u32[]{:S(2)}, u32[]{:S(2)}) %all-to-all-start.13) | async-done | bytes 786464 | tf_op jit(solution)/shard_map/all_to_all | solution.py:45
  486.5 24.1 %all-to-all-done.14 = bf16[64,3,2048]{2,1,0:T(4,128)(2,1)} async-done(((bf16[64,3,2048]{2,1,0:T(4,128)(2,1)}), bf16[64,3,2048]{2,1,0:T(4,128)(2,1)}, u32[]{:S(2)}, u32[]{:S(2)}) %all-to-all-start.14) | async-done | bytes 786464 | tf_op jit(solution)/shard_map/all_to_all | solution.py:52
  542.1 22.4 %all-to-all-done.16 = bf16[64,3,2048]{2,1,0:T(4,128)(2,1)} async-done(((bf16[64,3,2048]{2,1,0:T(4,128)(2,1)}), bf16[64,3,2048]{2,1,0:T(4,128)(2,1)}, u32[]{:S(2)}, u32[]{:S(2)}) %all-to-all-start.16) | async-done | bytes 786464 | tf_op jit(solution)/shard_map/all_to_all | solution.py:45
  580.6 26.7 %all-to-all-done.17 = bf16[64,3,2048]{2,1,0:T(4,128)(2,1)} async-done(((bf16[64,3,2048]{2,1,0:T(4,128)(2,1)}), bf16[64,3,2048]{2,1,0:T(4,128)(2,1)}, u32[]{:S(2)}, u32[]{:S(2)}) %all-to-all-start.17) | async-done | bytes 786464 | tf_op jit(solution)/shard_map/all_to_all | solution.py:52
  642.5 23.4 %all-to-all-done.19 = bf16[64,3,2048]{2,1,0:T(4,128)(2,1)} async-done(((bf16[64,3,2048]{2,1,0:T(4,128)(2,1)}), bf16[64,3,2048]{2,1,0:T(4,128)(2,1)}, u32[]{:S(2)}, u32[]{:S(2)}) %all-to-all-start.19) | async-done | bytes 786464 | tf_op jit(solution)/shard_map/all_to_all | solution.py:45
  701.7 20.6 %all-to-all-done.22 = bf16[64,3,2048]{2,1,0:T(4,128)(2,1)} async-done(((bf16[64,3,2048]{2,1,0:T(4,128)(2,1)}), bf16[64,3,2048]{2,1,0:T(4,128)(2,1)}, u32[]{:S(2)}, u32[]{:S(2)}) %all-to-all-start.22) | async-done | bytes 786464 | tf_op jit(solution)/shard_map/all_to_all | solution.py:60
  750.4 28.5 %all-to-all-done.23 = bf16[64,3,2048]{2,1,0:T(4,128)(2,1)} async-done(((bf16[64,3,2048]{2,1,0:T(4,128)(2,1)}), bf16[64,3,2048]{2,1,0:T(4,128)(2,1)}, u32[]{:S(2)}, u32[]{:S(2)}) %all-to-all-start.23) | async-done | bytes 786464 | tf_op jit(solution)/shard_map/all_to_all | solution.py:56
  788.4 19.0 %all-to-all-done.24 = bf16[64,3,2048]{2,1,0:T(4,128)(2,1)} async-done(((bf16[64,3,2048]{2,1,0:T(4,128)(2,1)}), bf16[64,3,2048]{2,1,0:T(4,128)(2,1)}, u32[]{:S(2)}, u32[]{:S(2)}) %all-to-all-start.24) | async-done | bytes 786464 | tf_op jit(solution)/shard_map/all_to_all | solution.py:60
  839.6 28.5 %all-to-all-done.25 = bf16[64,3,2048]{2,1,0:T(4,128)(2,1)} async-done(((bf16[64,3,2048]{2,1,0:T(4,128)(2,1)}), bf16[64,3,2048]{2,1,0:T(4,128)(2,1)}, u32[]{:S(2)}, u32[]{:S(2)}) %all-to-all-start.25) | async-done | bytes 786464 | tf_op jit(solution)/shard_map/all_to_all | solution.py:56
  877.8 19.0 %all-to-all-done.26 = bf16[64,3,2048]{2,1,0:T(4,128)(2,1)} async-done(((bf16[64,3,2048]{2,1,0:T(4,128)(2,1)}), bf16[64,3,2048]{2,1,0:T(4,128)(2,1)}, u32[]{:S(2)}, u32[]{:S(2)}) %all-to-all-start.26) | async-done | bytes 786464 | tf_op jit(solution)/shard_map/all_to_all | solution.py:60
  930.2 28.5 %all-to-all-done.27 = bf16[64,3,2048]{2,1,0:T(4,128)(2,1)} async-done(((bf16[64,3,2048]{2,1,0:T(4,128)(2,1)}), bf16[64,3,2048]{2,1,0:T(4,128)(2,1)}, u32[]{:S(2)}, u32[]{:S(2)}) %all-to-all-start.27) | async-done | bytes 786464 | tf_op jit(solution)/shard_map/all_to_all | solution.py:56
  976.9 19.1 %all-to-all-done.28 = bf16[64,3,2048]{2,1,0:T(4,128)(2,1)} async-done(((bf16[64,3,2048]{2,1,0:T(4,128)(2,1)}), bf16[64,3,2048]{2,1,0:T(4,128)(2,1)}, u32[]{:S(2)}, u32[]{:S(2)}) %all-to-all-start.28) | async-done | bytes 786464 | tf_op jit(solution)/shard_map/all_to_all | solution.py:60
  1020.2 28.5 %all-to-all-done.29 = bf16[64,3,2048]{2,1,0:T(4,128)(2,1)} async-done(((bf16[64,3,2048]{2,1,0:T(4,128)(2,1)}), bf16[64,3,2048]{2,1,0:T(4,128)(2,1)}, u32[]{:S(2)}, u32[]{:S(2)}) %all-to-all-start.29) | async-done | bytes 786464 | tf_op jit(solution)/shard_map/all_to_all | solution.py:56
  1066.9 19.1 %all-to-all-done.30 = bf16[64,3,2048]{2,1,0:T(4,128)(2,1)} async-done(((bf16[64,3,2048]{2,1,0:T(4,128)(2,1)}), bf16[64,3,2048]{2,1,0:T(4,128)(2,1)}, u32[]{:S(2)}, u32[]{:S(2)}) %all-to-all-start.30) | async-done | bytes 786464 | tf_op jit(solution)/shard_map/all_to_all | solution.py:60
  1091.4 23.4 %collective-permute-done.10 = bf16[32,2048]{1,0:T(8,128)(2,1)S(1)} collective-permute-done((bf16[32,2048]{1,0:T(8,128)(2,1)S(1)}, bf16[32,2048]{1,0:T(8,128)(2,1)S(1)}, u32[]{:S(2)}, u32[]{:S(2)}) %collective-permute-start.10) | collective-permute-done | bytes 131104 | tf_op jit(solution)/shard_map/ppermute | solution.py:13
  1123.6 28.0 %all-to-all-done.31 = bf16[64,3,2048]{2,1,0:T(4,128)(2,1)} async-done(((bf16[64,3,2048]{2,1,0:T(4,128)(2,1)}), bf16[64,3,2048]{2,1,0:T(4,128)(2,1)}, u32[]{:S(2)}, u32[]{:S(2)}) %all-to-all-start.31) | async-done | bytes 786464 | tf_op jit(solution)/shard_map/all_to_all | solution.py:56
  1170.2 27.8 %all-to-all-done.32 = bf16[64,3,2048]{2,1,0:T(4,128)(2,1)} async-done(((bf16[64,3,2048]{2,1,0:T(4,128)(2,1)}), bf16[64,3,2048]{2,1,0:T(4,128)(2,1)}, u32[]{:S(2)}, u32[]{:S(2)}) %all-to-all-start.32) | async-done | bytes 786464 | tf_op jit(solution)/shard_map/all_to_all | solution.py:60
  1302.3 111.4 %all-gather = f32[131072]{0:T(1024)S(1)} all-gather(f32[2048]{0:T(1024)S(1)} %add_add_fusion), channel_id=2, replica_groups=mesh['dp'=8,'pipe'=4,'expert'=8] {'dp','expert'}, dimensions={0}, use_global_device_ids=true | all-gather | bytes 532480 | tf_op jit(solution)/shard_map/all_gather | solution.py:226
  (418 shorter events, 826.7 us)
Async XLA Ops:
  5.5 27.2 %all-to-all-start = ((bf16[64,3,1]{1,2,0:T(2,128)(2,1)}), bf16[64,3,1]{1,2,0:T(2,128)(2,1)S(1)}, u32[]{:S(2)}, u32[]{:S(2)}) async-start(bf16[64,3,1]{1,2,0:T(2,128)(2,1)} %copy.214), calls=%async_computation | async-start | bytes 65536 | tf_op jit(solution)/shard_map/all_to_all | solution.py:46
  32.7 33.2 %all-to-all-start.1 = ((bf16[64,3,2048]{2,1,0:T(4,128)(2,1)}), bf16[64,3,2048]{2,1,0:T(4,128)(2,1)}, u32[]{:S(2)}, u32[]{:S(2)}) async-start(bf16[64,3,2048]{2,1,0:T(4,128)(2,1)} %copy.215), calls=%async_computation.1 | async-start | bytes 2097152 | tf_op jit(solution)/shard_map/all_to_all | solution.py:45
  78.3 24.5 %all-to-all-start.2 = ((bf16[64,3,2048]{2,1,0:T(4,128)(2,1)}), bf16[64,3,2048]{2,1,0:T(4,128)(2,1)}, u32[]{:S(2)}, u32[]{:S(2)}) async-start(bf16[64,3,2048]{2,1,0:T(4,128)(2,1)} %reshape.730), calls=%async_computation.2 | async-start | bytes 2097152 | tf_op jit(solution)/shard_map/all_to_all | solution.py:52
  122.4 43.0 %all-to-all-start.4 = ((bf16[64,3,2048]{2,1,0:T(4,128)(2,1)}), bf16[64,3,2048]{2,1,0:T(4,128)(2,1)}, u32[]{:S(2)}, u32[]{:S(2)}) async-start(bf16[64,3,2048]{2,1,0:T(4,128)(2,1)} %copy.219), calls=%async_computation.4 | async-start | bytes 2097152 | tf_op jit(solution)/shard_map/all_to_all | solution.py:45
  240.8 34.5 %all-to-all-start.7 = ((bf16[64,3,2048]{2,1,0:T(4,128)(2,1)}), bf16[64,3,2048]{2,1,0:T(4,128)(2,1)}, u32[]{:S(2)}, u32[]{:S(2)}) async-start(bf16[64,3,2048]{2,1,0:T(4,128)(2,1)} %copy.223), calls=%async_computation.7 | async-start | bytes 2097152 | tf_op jit(solution)/shard_map/all_to_all | solution.py:45
  287.7 31.1 %all-to-all-start.8 = ((bf16[64,3,2048]{2,1,0:T(4,128)(2,1)}), bf16[64,3,2048]{2,1,0:T(4,128)(2,1)}, u32[]{:S(2)}, u32[]{:S(2)}) async-start(bf16[64,3,2048]{2,1,0:T(4,128)(2,1)} %reshape.734), calls=%async_computation.8 | async-start | bytes 2097152 | tf_op jit(solution)/shard_map/all_to_all | solution.py:52
  345.1 32.7 %all-to-all-start.10 = ((bf16[64,3,2048]{2,1,0:T(4,128)(2,1)}), bf16[64,3,2048]{2,1,0:T(4,128)(2,1)}, u32[]{:S(2)}, u32[]{:S(2)}) async-start(bf16[64,3,2048]{2,1,0:T(4,128)(2,1)} %copy.227), calls=%async_computation.10 | async-start | bytes 2097152 | tf_op jit(solution)/shard_map/all_to_all | solution.py:45
  390.2 31.1 %all-to-all-start.11 = ((bf16[64,3,2048]{2,1,0:T(4,128)(2,1)}), bf16[64,3,2048]{2,1,0:T(4,128)(2,1)}, u32[]{:S(2)}, u32[]{:S(2)}) async-start(bf16[64,3,2048]{2,1,0:T(4,128)(2,1)} %reshape.736), calls=%async_computation.11 | async-start | bytes 2097152 | tf_op jit(solution)/shard_map/all_to_all | solution.py:52
  447.0 27.6 %all-to-all-start.13 = ((bf16[64,3,2048]{2,1,0:T(4,128)(2,1)}), bf16[64,3,2048]{2,1,0:T(4,128)(2,1)}, u32[]{:S(2)}, u32[]{:S(2)}) async-start(bf16[64,3,2048]{2,1,0:T(4,128)(2,1)} %copy.231), calls=%async_computation.13 | async-start | bytes 2097152 | tf_op jit(solution)/shard_map/all_to_all | solution.py:45
  479.9 30.7 %all-to-all-start.14 = ((bf16[64,3,2048]{2,1,0:T(4,128)(2,1)}), bf16[64,3,2048]{2,1,0:T(4,128)(2,1)}, u32[]{:S(2)}, u32[]{:S(2)}) async-start(bf16[64,3,2048]{2,1,0:T(4,128)(2,1)} %reshape.738), calls=%async_computation.14 | async-start | bytes 2097152 | tf_op jit(solution)/shard_map/all_to_all | solution.py:52
  536.3 28.2 %all-to-all-start.16 = ((bf16[64,3,2048]{2,1,0:T(4,128)(2,1)}), bf16[64,3,2048]{2,1,0:T(4,128)(2,1)}, u32[]{:S(2)}, u32[]{:S(2)}) async-start(bf16[64,3,2048]{2,1,0:T(4,128)(2,1)} %copy.235), calls=%async_computation.16 | async-start | bytes 2097152 | tf_op jit(solution)/shard_map/all_to_all | solution.py:45
  569.6 37.7 %all-to-all-start.17 = ((bf16[64,3,2048]{2,1,0:T(4,128)(2,1)}), bf16[64,3,2048]{2,1,0:T(4,128)(2,1)}, u32[]{:S(2)}, u32[]{:S(2)}) async-start(bf16[64,3,2048]{2,1,0:T(4,128)(2,1)} %reshape.740), calls=%async_computation.17 | async-start | bytes 2097152 | tf_op jit(solution)/shard_map/all_to_all | solution.py:52
  631.6 34.4 %all-to-all-start.19 = ((bf16[64,3,2048]{2,1,0:T(4,128)(2,1)}), bf16[64,3,2048]{2,1,0:T(4,128)(2,1)}, u32[]{:S(2)}, u32[]{:S(2)}) async-start(bf16[64,3,2048]{2,1,0:T(4,128)(2,1)} %copy.239), calls=%async_computation.19 | async-start | bytes 2097152 | tf_op jit(solution)/shard_map/all_to_all | solution.py:45
  694.6 27.6 %all-to-all-start.22 = ((bf16[64,3,2048]{2,1,0:T(4,128)(2,1)}), bf16[64,3,2048]{2,1,0:T(4,128)(2,1)}, u32[]{:S(2)}, u32[]{:S(2)}) async-start(bf16[64,3,2048]{2,1,0:T(4,128)(2,1)} %reshape.745), calls=%async_computation.22 | async-start | bytes 2097152 | tf_op jit(solution)/shard_map/all_to_all | solution.py:60
  744.6 34.2 %all-to-all-start.23 = ((bf16[64,3,2048]{2,1,0:T(4,128)(2,1)}), bf16[64,3,2048]{2,1,0:T(4,128)(2,1)}, u32[]{:S(2)}, u32[]{:S(2)}) async-start(bf16[64,3,2048]{2,1,0:T(4,128)(2,1)} %copy.251), calls=%async_computation.23 | async-start | bytes 2097152 | tf_op jit(solution)/shard_map/all_to_all | solution.py:56
  827.4 40.7 %all-to-all-start.25 = ((bf16[64,3,2048]{2,1,0:T(4,128)(2,1)}), bf16[64,3,2048]{2,1,0:T(4,128)(2,1)}, u32[]{:S(2)}, u32[]{:S(2)}) async-start(bf16[64,3,2048]{2,1,0:T(4,128)(2,1)} %copy.253), calls=%async_computation.25 | async-start | bytes 2097152 | tf_op jit(solution)/shard_map/all_to_all | solution.py:56
  922.4 36.3 %all-to-all-start.27 = ((bf16[64,3,2048]{2,1,0:T(4,128)(2,1)}), bf16[64,3,2048]{2,1,0:T(4,128)(2,1)}, u32[]{:S(2)}, u32[]{:S(2)}) async-start(bf16[64,3,2048]{2,1,0:T(4,128)(2,1)} %copy.255), calls=%async_computation.27 | async-start | bytes 2097152 | tf_op jit(solution)/shard_map/all_to_all | solution.py:56
  1012.4 36.3 %all-to-all-start.29 = ((bf16[64,3,2048]{2,1,0:T(4,128)(2,1)}), bf16[64,3,2048]{2,1,0:T(4,128)(2,1)}, u32[]{:S(2)}, u32[]{:S(2)}) async-start(bf16[64,3,2048]{2,1,0:T(4,128)(2,1)} %copy.257), calls=%async_computation.29 | async-start | bytes 2097152 | tf_op jit(solution)/shard_map/all_to_all | solution.py:56
  1090.1 24.7 %collective-permute-start.10 = (bf16[32,2048]{1,0:T(8,128)(2,1)S(1)}, bf16[32,2048]{1,0:T(8,128)(2,1)S(1)}, u32[]{:S(2)}, u32[]{:S(2)}) collective-permute-start(bf16[32,2048]{1,0:T(8,128)(2,1)S(1)} %get-tuple-element.782), channel_id=1, source_target_pairs={{8,0},{16,8},{24,16},{9,1},{17,9},{25,17},{10,2},{18,10},{26,18},{... | collective-permute-start | bytes 393224 | tf_op jit(solution)/shard_map/ppermute | solution.py:13
  1117.9 33.7 %all-to-all-start.31 = ((bf16[64,3,2048]{2,1,0:T(4,128)(2,1)}), bf16[64,3,2048]{2,1,0:T(4,128)(2,1)}, u32[]{:S(2)}, u32[]{:S(2)}) async-start(bf16[64,3,2048]{2,1,0:T(4,128)(2,1)} %copy.259), calls=%async_computation.31 | async-start | bytes 2097152 | tf_op jit(solution)/shard_map/all_to_all | solution.py:56
  1164.6 33.5 %all-to-all-start.32 = ((bf16[64,3,2048]{2,1,0:T(4,128)(2,1)}), bf16[64,3,2048]{2,1,0:T(4,128)(2,1)}, u32[]{:S(2)}, u32[]{:S(2)}) async-start(bf16[64,3,2048]{2,1,0:T(4,128)(2,1)} %reshape.755), calls=%async_computation.32 | async-start | bytes 2097152 | tf_op jit(solution)/shard_map/all_to_all | solution.py:60
  1211.5 31.9 %all-to-all-start.33 = ((bf16[64,3,2048]{2,1,0:T(4,128)(2,1)}), bf16[64,3,2048]{2,1,0:T(4,128)(2,1)}, u32[]{:S(2)}, u32[]{:S(2)}) async-start(bf16[64,3,2048]{2,1,0:T(4,128)(2,1)} %copy.261), calls=%async_computation.33 | async-start | bytes 2097152 | tf_op jit(solution)/shard_map/all_to_all | solution.py:56
  1243.3 29.7 %all-to-all-start.20 = ((bf16[64,3,2048]{2,1,0:T(4,128)(2,1)}), bf16[64,3,2048]{2,1,0:T(4,128)(2,1)}, u32[]{:S(2)}, u32[]{:S(2)}) async-start(bf16[64,3,2048]{2,1,0:T(4,128)(2,1)} %reshape.742), calls=%async_computation.20 | async-start | bytes 2097152 | tf_op jit(solution)/shard_map/all_to_all | solution.py:52
  1273.1 27.3 %all-to-all-start.34 = ((bf16[64,3,2048]{2,1,0:T(4,128)(2,1)}), bf16[64,3,2048]{2,1,0:T(4,128)(2,1)S(1)}, u32[]{:S(2)}, u32[]{:S(2)}) async-start(bf16[64,3,2048]{2,1,0:T(4,128)(2,1)} %reshape.757), calls=%async_computation.34 | async-start | bytes 2097152 | tf_op jit(solution)/shard_map/all_to_all | solution.py:60
  (51 other events, 742.1 us)
